TPU v7x, 32 devices: a whole 2x2x4 slice. The times are simulated.
32 devices in a mesh: groups: 2 (over y), view: 4 (over z), row: 4 (over x, core).
Axes of the slice: x: 2, y: 2, z: 4, core: 2. Of those that a mesh axis runs over, the one named last changes fastest.
Arguments:
- inputs: bfloat16 [64, 292, 16, 16], P(None, 'view', ('groups', 'row')), parts along dimension 2, may hold values from -24 to 24
- cotangent: bfloat16 [64, 292, 16, 16], P(None, None, ('groups', 'row'), 'view'), parts along dimension 2, may hold values from -6 to 6
- keep: int32 [584], P('groups'), parts along dimension 0, may hold values from 0 to 1, as said below
- w_conv: bfloat16 [64, 64, 3, 3], replicated, may hold values from -0.25 to 0.25
- gain: float32 [64], replicated, may hold values from 0.5 to 1.5
- w_query: bfloat16 [64, 64], replicated, may hold values from -3 to 3
- w_key: bfloat16 [64, 64], replicated, may hold values from -3 to 3
- w_value: bfloat16 [64, 64], replicated, may hold values from -0.75 to 0.75
- w_out: bfloat16 [64, 64], replicated, may hold values from -0.75 to 0.75
Outputs:
- output: bfloat16 [64, 292, 16, 16], P(None, None, ('groups', 'row'), 'view'), parts along dimension 2
- d_input: bfloat16 [64, 292, 16, 16], P(None, 'view', ('groups', 'row')), parts along dimension 2
- g_conv: float32 [128, 64, 3, 3], P('groups'), parts along dimension 0
- g_gain: float32 [128], P('groups'), parts along dimension 0
- g_query: float32 [128, 64], P('groups'), parts along dimension 0
- g_key: float32 [128, 64], P('groups'), parts along dimension 0
- g_value: float32 [128, 64], P('groups'), parts along dimension 0
- g_out: float32 [128, 64], P('groups'), parts along dimension 0
There are 2 independent parts, one for each index of `groups`. A program takes and returns all parts, laid end to end along the dimension named above; an argument that names none is the same for every part. Nothing has to cross between parts.
Inputs may be any that keep to these rules, and one draw needn't show every extreme that they name: `keep`: zero at every view from 289 on, one at view 289 // 2.
All inputs are finite; a program needn't handle non-finite values.
Results may differ from a plain program's by a relative error of at most 0.012.
The roundings to bfloat16 on the way count: a program that leaves them out, or rounds other values in their place, can miss the bound.
Values may be sent and summed in bfloat16 or wider, within the bound.
No kernel may reach another device: no remote copies, remote signals or barrier semaphores. Data moves between devices by JAX's collectives and lax.ppermute only.
A program may use at most 64 MiB of HBM per device.

v0:
```python
import math
import jax
import jax.numpy as jnp
from jax import lax
from jax.sharding import PartitionSpec as P


def with_halo(cells, sides, width):
    for axis, dim in sides:
        count = lax.axis_size(axis)
        ends = count - 1
        head = lax.slice_in_dim(cells, 0, width, axis=dim)
        tail = lax.slice_in_dim(cells, cells.shape[dim] - width, cells.shape[dim], axis=dim)
        cells = jnp.concatenate(
            [
                lax.ppermute(tail, axis, [(i, (i + 1) % count) for i in range(ends)]),
                cells,
                lax.ppermute(head, axis, [((i + 1) % count, i) for i in range(ends)]),
            ],
            axis=dim,
        )
    return cells


def product(form, left, right):
    return jnp.einsum(form, left, right, preferred_element_type=jnp.float32)


def convolve(padded, w_conv):
    height = padded.shape[2] - 2
    breadth = padded.shape[3] - 2
    total = jnp.zeros((w_conv.shape[0], padded.shape[1], height, breadth), jnp.float32)
    for row_tap in range(3):
        for col_tap in range(3):
            window = padded[:, :, row_tap : row_tap + height, col_tap : col_tap + breadth]
            total = total + product("oc,cvrw->ovrw", w_conv[:, :, row_tap, col_tap], window)
    return total


def input_grad(grad_pad, w_conv):
    height = grad_pad.shape[2] - 2
    breadth = grad_pad.shape[3] - 2
    total = jnp.zeros((w_conv.shape[1], grad_pad.shape[1], height, breadth), jnp.float32)
    for row_tap in range(3):
        for col_tap in range(3):
            window = grad_pad[
                :, :, 2 - row_tap : 2 - row_tap + height, 2 - col_tap : 2 - col_tap + breadth
            ]
            total = total + product("oc,ovrw->cvrw", w_conv[:, :, row_tap, col_tap], window)
    return total


def weight_grad(grad, padded):
    height = grad.shape[2]
    breadth = grad.shape[3]
    taps = []
    for row_tap in range(3):
        for col_tap in range(3):
            window = padded[:, :, row_tap : row_tap + height, col_tap : col_tap + breadth]
            taps.append(product("ovrw,cvrw->oc", grad, window))
    stacked = jnp.stack(taps, axis=2)
    return stacked.reshape(grad.shape[0], padded.shape[0], 3, 3)


def angular(mixed_in, grad_out, keep, gain, w_query, w_key, w_value, w_out, used):
    pixels, all_views, channels = mixed_in.shape
    scale = 1.0 / math.sqrt(channels)
    values = mixed_in.astype(jnp.float32)
    centred = values - jnp.mean(values, axis=2, keepdims=True)
    rstd = lax.rsqrt(jnp.mean(centred * centred, axis=2, keepdims=True) + 1e-05)
    normed = centred * rstd
    normal_in = (normed * gain[None, None, :]).astype(jnp.bfloat16)
    query = product("cd,pvc->pvd", w_query, normal_in).astype(jnp.bfloat16)
    key_proj = product("cd,pvc->pvd", w_key, normal_in).astype(jnp.bfloat16)
    value_proj = product("cd,pvc->pvd", w_value, normal_in).astype(jnp.bfloat16)
    scores = product("pvd,pud->pvu", query, key_proj) * scale
    scores = jnp.where(keep[None, None, :used] > 0, scores, -1e30)
    highest = jnp.max(scores, axis=2, keepdims=True)
    expo = jnp.exp(scores - highest)
    probs = expo / jnp.sum(expo, axis=2, keepdims=True)
    probs_b = probs.astype(jnp.bfloat16)
    attended = product("pvu,pud->pvd", probs_b, value_proj).astype(jnp.bfloat16)
    output = (values + product("dc,pvd->pvc", w_out, attended)).astype(jnp.bfloat16)
    d_attended = product("dc,pvc->pvd", w_out, grad_out).astype(jnp.bfloat16)
    g_out = product("pvd,pvc->dc", attended, grad_out)
    d_probs = product("pvd,pud->pvu", d_attended, value_proj)
    d_value = product("pvu,pvd->pud", probs_b, d_attended).astype(jnp.bfloat16)
    inner = jnp.sum(probs * d_probs, axis=2, keepdims=True)
    d_scores = (probs * (d_probs - inner) * scale).astype(jnp.bfloat16)
    d_query = product("pvu,pud->pvd", d_scores, key_proj).astype(jnp.bfloat16)
    d_key = product("pvu,pvd->pud", d_scores, query).astype(jnp.bfloat16)
    g_query = product("pvc,pvd->cd", normal_in, d_query)
    g_key = product("pvc,pvd->cd", normal_in, d_key)
    g_value = product("pvc,pvd->cd", normal_in, d_value)
    d_normal = (
        product("cd,pvd->pvc", w_query, d_query)
        + product("cd,pvd->pvc", w_key, d_key)
        + product("cd,pvd->pvc", w_value, d_value)
    )
    g_gain = jnp.sum(d_normal * normed, axis=(0, 1))
    scaled = d_normal * gain[None, None, :]
    back = (
        scaled
        - jnp.mean(scaled, axis=2, keepdims=True)
        - normed * jnp.mean(scaled * normed, axis=2, keepdims=True)
    )
    d_spatial = (grad_out.astype(jnp.float32) + back * rstd).astype(jnp.bfloat16)
    return (output, d_spatial, (g_gain, g_query, g_key, g_value, g_out))


def angular_rows(spatial, cotangent, keep, gain, w_query, w_key, w_value, w_out, used):

    def row_pass(pair):
        return angular(pair[0], pair[1], keep, gain, w_query, w_key, w_value, w_out, used)

    spatial_last = jnp.transpose(spatial, (2, 3, 1, 0))
    cotangent_last = jnp.transpose(cotangent, (2, 3, 1, 0))
    out_rows, grad_rows, grads = lax.map(row_pass, (spatial_last, cotangent_last))
    summed = tuple((jnp.sum(item, axis=0) for item in grads))
    return (jnp.transpose(out_rows, (3, 2, 0, 1)), jnp.transpose(grad_rows, (3, 2, 0, 1)), summed)


def body(inputs, cotangent, keep, w_conv, gain, w_query, w_key, w_value, w_out):
    channels, view_dev, row_dev, width = inputs.shape
    blocks = lax.axis_size("view")
    breadth = width // blocks
    all_views = view_dev * blocks
    padded = with_halo(inputs, (("row", 2),), 1)
    padded = jnp.pad(padded, ((0, 0), (0, 0), (0, 0), (1, 1)))
    spatial = (inputs.astype(jnp.float32) + convolve(padded, w_conv)).astype(jnp.bfloat16)
    moved = lax.all_to_all(
        spatial.reshape(channels, view_dev, row_dev, blocks, breadth),
        "view",
        split_axis=3,
        concat_axis=1,
        tiled=True,
    )
    moved = moved.reshape(channels, all_views, row_dev, breadth)
    output, d_spatial, grads = angular_rows(
        moved, cotangent, keep, gain, w_query, w_key, w_value, w_out, all_views
    )
    returned = lax.all_to_all(
        d_spatial.reshape(channels, all_views, row_dev, 1, breadth),
        "view",
        split_axis=1,
        concat_axis=3,
        tiled=True,
    )
    returned = returned.reshape(channels, view_dev, row_dev, width)
    grad_pad = with_halo(returned, (("row", 2),), 1)
    grad_pad = jnp.pad(grad_pad, ((0, 0), (0, 0), (0, 0), (1, 1)))
    d_input = (returned.astype(jnp.float32) + input_grad(grad_pad, w_conv)).astype(jnp.bfloat16)
    g_conv = weight_grad(returned, padded)
    g_gain, g_query, g_key, g_value, g_out = grads
    g_conv, g_gain, g_query, g_key, g_value, g_out = lax.psum(
        (g_conv, g_gain, g_query, g_key, g_value, g_out), ("view", "row")
    )
    return (output, d_input, g_conv, g_gain, g_query, g_key, g_value, g_out)


def solution(mesh):
    placed = (
        P(None, "view", ("groups", "row"), None),
        P(None, None, ("groups", "row"), "view"),
        P("groups"),
        P(),
        P(),
        P(),
        P(),
        P(),
        P(),
    )
    return jax.shard_map(
        body,
        mesh=mesh,
        in_specs=placed,
        out_specs=(
            P(None, None, ("groups", "row"), "view"),
            P(None, "view", ("groups", "row"), None),
            P("groups", None, None, None),
            P("groups"),
            P("groups", None),
            P("groups", None),
            P("groups", None),
            P("groups", None),
        ),
        check_vma=False,
    )
```

profile of v0, /device:TPU:0, one launch (start us, length us, event | category | flops | bytes accessed | tf_op | source)
XLA Modules:
  0.0 311.2 jit_solution(1073874773569292355)
XLA Ops:
  8.4 2.4 collective-permute-start
  13.2 3.2 %collective-permute-done.1 = bf16[64,73,1,16]{1,0,3,2:T(8,128)(2,1)S(1)} collective-permute-done((bf16[64,73,1,16]{1,0,3,2:T(8,128)(2,1)S(1)}, bf16[64,73,1,16]{1,0,3,2:T(8,128)(2,1)S(1)}, u32[]{:S(2)}, u32[]{:S(2)}) %collective-permute-start.1) | collective-permute-done | bytes 149536 | tf_op jit(solution)/shard_map/ppermute | solution.py:18
  20.0 5.0 %all-to-all-start = ((bf16[64,73,2,4,4]{1,0,4,2,3:T(8,128)(2,1)}), bf16[64,73,2,4,4]{1,0,4,2,3:T(8,128)(2,1)S(1)}, u32[]{:S(2)}, u32[]{:S(2)}) async-start(bf16[64,73,2,4,4]{1,0,4,2,3:T(8,128)(2,1)} %copy.93), calls=%async_computation | async-start | bytes 1048576 | tf_op jit(solution)/shard_map/all_to_all | solution.py:131
  25.1 12.3 %all-to-all-done = bf16[64,73,2,4,4]{1,0,4,2,3:T(8,128)(2,1)S(1)} async-done(((bf16[64,73,2,4,4]{1,0,4,2,3:T(8,128)(2,1)}), bf16[64,73,2,4,4]{1,0,4,2,3:T(8,128)(2,1)S(1)}, u32[]{:S(2)}, u32[]{:S(2)}) %all-to-all-start) | async-done | bytes 299040 | tf_op jit(solution)/shard_map/all_to_all | solution.py:131
  38.2 56.6 %while.22 = (s32[]{:T(128)}, bf16[2,4,292,64]{2,1,0,3:T(4,128)(2,1)}, bf16[2,4,292,64]{2,3,1,0:T(8,128)(2,1)}, f32[2,64]{1,0:T(2,128)}, f32[2,64,64]{2,1,0:T(8,1...) while((s32[]{:T(128)}, ...), condition=%wide.region_9.10_spmd, body=%wide.region_0.9_spmd.sunk | while | flops 399432576 | bytes 35407752 | solution.py:118
  41.3 1.6 convolution_convert_fusion.12
  42.9 3.1 %fusion.288 = (f32[4,292]{1,0:T(4,128)S(1)}, f32[4,292,292]{1,2,0:T(8,128)}) fusion(pred[292]{0:T(512)(128)(4,1)S(1)} %broadcast_compare_fusion.2, bf16[4,292,64]{1,2,0:T(8,128)(2,1)} %convolution_convert_fusion.12, bf16[64,64]{1,0:T(8,128)(2,1)S(1)} %copy-done.17, f32[64]{0:T(128)} %get-tuple-element.425, f32[4,292]{1,0:T(4,128)S(1)} %add_rsqrt_fusion.2, ...), kind=kOutput, calls=%fused_computation.193.clone.1 | convolution fusion | flops 55036452 | bytes 1744452 | tf_op jit(solution)/shard_map/while/body/eval_jaxpr/sub | solution.py:79
  46.0 3.5 %fusion.293 = bf16[4,292,64]{1,2,0:T(8,128)(2,1)} fusion(f32[4,292,292]{1,2,0:T(8,128)S(1)} %fusion.290, f32[4,292,292]{1,2,0:T(8,128)} %get-tuple-element.288, f32[4,292]{1,0:T(4,128)S(1)} %get-tuple-element.289, bf16[64,64]{1,0:T(8,128)(2,1)S(1)} %copy-done.17, f32[64]{0:T(128)} %get-tuple-element.425, f32[4,292]{1,0:T(4,128)S(1)} %add_rsqrt_fusion.2, ...), kind=kOutput, calls=%fused_computation.14.clone.1 | convolution fusion | flops 56135540 | bytes 7662592 | tf_op jit(solution)/shard_map/while/body/eval_jaxpr/pvu,pvd->pud/dot_general | solution.py:26
  49.6 3.5 %fusion.291 = bf16[4,292,64]{1,2,0:T(8,128)(2,1)} fusion(bf16[4,292,64]{1,2,0:T(8,128)(2,1)} %convolution_convert_fusion.12, f32[4,292,292]{1,2,0:T(8,128)S(1)} %fusion.290, f32[4,292,292]{1,2,0:T(8,128)} %get-tuple-element.288, f32[4,292]{1,0:T(4,128)S(1)} %get-tuple-element.289), kind=kOutput, calls=%fused_computation.13.clone.1 | convolution fusion | flops 46118772 | bytes 3032128 | tf_op jit(solution)/shard_map/while/body/eval_jaxpr/pvu,pud->pvd/dot_general | solution.py:26
  55.3 2.0 convolution_convert_fusion.15
  62.5 1.9 convolution_convert_fusion.13
  69.6 1.6 convolution_convert_fusion.12
  71.2 3.1 %fusion.288 = (f32[4,292]{1,0:T(4,128)S(1)}, f32[4,292,292]{1,2,0:T(8,128)}) fusion(pred[292]{0:T(512)(128)(4,1)S(1)} %broadcast_compare_fusion.2, bf16[4,292,64]{1,2,0:T(8,128)(2,1)} %convolution_convert_fusion.12, bf16[64,64]{1,0:T(8,128)(2,1)S(1)} %copy-done.17, f32[64]{0:T(128)} %get-tuple-element.425, f32[4,292]{1,0:T(4,128)S(1)} %add_rsqrt_fusion.2, ...), kind=kOutput, calls=%fused_computation.193.clone.1 | convolution fusion | flops 55036452 | bytes 1744452 | tf_op jit(solution)/shard_map/while/body/eval_jaxpr/sub | solution.py:79
  74.3 3.5 %fusion.293 = bf16[4,292,64]{1,2,0:T(8,128)(2,1)} fusion(f32[4,292,292]{1,2,0:T(8,128)S(1)} %fusion.290, f32[4,292,292]{1,2,0:T(8,128)} %get-tuple-element.288, f32[4,292]{1,0:T(4,128)S(1)} %get-tuple-element.289, bf16[64,64]{1,0:T(8,128)(2,1)S(1)} %copy-done.17, f32[64]{0:T(128)} %get-tuple-element.425, f32[4,292]{1,0:T(4,128)S(1)} %add_rsqrt_fusion.2, ...), kind=kOutput, calls=%fused_computation.14.clone.1 | convolution fusion | flops 56135540 | bytes 7662592 | tf_op jit(solution)/shard_map/while/body/eval_jaxpr/pvu,pvd->pud/dot_general | solution.py:26
  77.9 3.5 %fusion.291 = bf16[4,292,64]{1,2,0:T(8,128)(2,1)} fusion(bf16[4,292,64]{1,2,0:T(8,128)(2,1)} %convolution_convert_fusion.12, f32[4,292,292]{1,2,0:T(8,128)S(1)} %fusion.290, f32[4,292,292]{1,2,0:T(8,128)} %get-tuple-element.288, f32[4,292]{1,0:T(4,128)S(1)} %get-tuple-element.289), kind=kOutput, calls=%fused_computation.13.clone.1 | convolution fusion | flops 46118772 | bytes 3032128 | tf_op jit(solution)/shard_map/while/body/eval_jaxpr/pvu,pud->pvd/dot_general | solution.py:26
  83.6 2.0 convolution_convert_fusion.15
  90.8 1.9 convolution_convert_fusion.13
  94.8 1.6 copy.97
  97.8 5.2 %all-to-all-start.1 = ((bf16[4,2,18688]{2,1,0:T(2,128)(2,1)}), bf16[4,2,18688]{2,1,0:T(2,128)(2,1)S(1)}, u32[]{:S(2)}, u32[]{:S(2)}) async-start(bf16[4,2,18688]{2,1,0:T(2,128)(2,1)} %reshape.106), calls=%async_computation.1 | async-start | bytes 598016 | tf_op jit(solution)/shard_map/all_to_all | solution.py:142
  106.3 6.2 %all-to-all-done.1 = bf16[4,2,18688]{2,1,0:T(2,128)(2,1)S(1)} async-done(((bf16[4,2,18688]{2,1,0:T(2,128)(2,1)}), bf16[4,2,18688]{2,1,0:T(2,128)(2,1)S(1)}, u32[]{:S(2)}, u32[]{:S(2)}) %all-to-all-start.1) | async-done | bytes 299040 | tf_op jit(solution)/shard_map/all_to_all | solution.py:142
  118.7 4.0 %collective-permute-start.2 = (bf16[64,73,1,16]{1,0,3,2:T(8,128)(2,1)S(1)}, bf16[64,73,1,16]{1,0,3,2:T(8,128)(2,1)S(1)}, u32[]{:S(2)}, u32[]{:S(2)}) collective-permute-start(bf16[64,73,1,16]{1,0,3,2:T(8,128)(2,1)S(1)} %get-tuple-element.172), channel_id=1, source_target_pairs={{0,1},{1,2},{2,3},{4,5},{5,6},{6,7},{8,9},{9,10},{10,11},{12,13},{... | collective-permute-start | bytes 448520 | tf_op jit(solution)/shard_map/ppermute | solution.py:16
  127.6 71.4 %all-reduce.8.cloned.1.call-done = (f32[64]{0:T(128)}, f32[64,64]{1,0:T(8,128)}, f32[64,64]{1,0:T(8,128)}, f32[64,64]{1,0:T(8,128)}, f32[64,64]{1,0:T(8,128)}) async-done(((f32[64]{0:T(128)}, f32[64,64]{1,0:T(8,128)}, f32[64,64]{1,0:T(8,128)}, f32[64,64]{1,0:T(8,128)}, f32[64,64]{1,0:T(8,128)}), (f32[64]{0:T(128)}, f32[64,64]{1,0:T(8,128)}, f32[64,64]{1,0:T(8,128)}, f32[64,64]{1,0:T(8,128)}, ...) | async-done | bytes 65808 | tf_op jit(solution)/shard_map/psum | solution.py:155
  199.0 97.0 %all-reduce.6.cloned.1.call-done = f32[64,64,3,3]{1,0,3,2:T(8,128)} async-done(((f32[64,64,3,3]{1,0,3,2:T(8,128)}), f32[64,64,3,3]{1,0,3,2:T(8,128)}) %all-reduce.6.cloned.1.call-update) | async-done | bytes 147472 | tf_op jit(solution)/shard_map/psum | solution.py:155
  296.0 1.7 copy.226
  (251 shorter events, 54.5 us)
Async XLA Ops:
  8.4 4.1 %collective-permute-start = (bf16[64,73,1,16]{1,0,3,2:T(8,128)(2,1)S(1)}, bf16[64,73,1,16]{1,0,3,2:T(8,128)(2,1)S(1)}, u32[]{:S(2)}, u32[]{:S(2)}) collective-permute-start(bf16[64,73,1,16]{1,0,3,2:T(8,128)(2,1)S(1)} %copy.172), channel_id=1, source_target_pairs={{0,1},{1,2},{2,3},{4,5},{5,6},{6,7},{8,9},{9,10},{10,11},{12,13},{... | collective-permute-start | bytes 448520 | tf_op jit(solution)/shard_map/ppermute | solution.py:16
  10.9 5.5 %collective-permute-start.1 = (bf16[64,73,1,16]{1,0,3,2:T(8,128)(2,1)S(1)}, bf16[64,73,1,16]{1,0,3,2:T(8,128)(2,1)S(1)}, u32[]{:S(2)}, u32[]{:S(2)}) collective-permute-start(bf16[64,73,1,16]{1,0,3,2:T(8,128)(2,1)S(1)} %copy.173), channel_id=1, source_target_pairs={{1,0},{2,1},{3,2},{5,4},{6,5},{7,6},{9,8},{10,9},{11,10},{13,12},{... | collective-permute-start | bytes 448520 | tf_op jit(solution)/shard_map/ppermute | solution.py:18
  19.1 5.9 %copy-start.18 = (bf16[64,292,2,4]{1,3,2,0:T(4,128)(2,1)S(1)}, bf16[64,292,2,4]{1,3,2,0:T(4,128)(2,1)}, u32[]{:S(2)}) copy-start(bf16[64,292,2,4]{1,3,2,0:T(4,128)(2,1)} %param.12) | copy-start | bytes 897028
  20.0 18.2 %copy-start.12 = (bf16[64,64]{1,0:T(8,128)(2,1)S(1)}, bf16[64,64]{1,0:T(8,128)(2,1)}, u32[]{:S(2)}) copy-start(bf16[64,64]{1,0:T(8,128)(2,1)} %param.19) | copy-start | bytes 24580
  20.0 18.2 %copy-start.15 = (bf16[64,64]{1,0:T(8,128)(2,1)S(1)}, bf16[64,64]{1,0:T(8,128)(2,1)}, u32[]{:S(2)}) copy-start(bf16[64,64]{1,0:T(8,128)(2,1)} %param.18) | copy-start | bytes 24580
  20.0 18.2 %copy-start.34 = (f32[64]{0:T(128)S(1)}, f32[64]{0:T(128)}, u32[]{:S(2)}) copy-start(f32[64]{0:T(128)} %param.15) | copy-start | bytes 772
  20.0 17.4 %all-to-all-start = ((bf16[64,73,2,4,4]{1,0,4,2,3:T(8,128)(2,1)}), bf16[64,73,2,4,4]{1,0,4,2,3:T(8,128)(2,1)S(1)}, u32[]{:S(2)}, u32[]{:S(2)}) async-start(bf16[64,73,2,4,4]{1,0,4,2,3:T(8,128)(2,1)} %copy.93), calls=%async_computation | async-start | bytes 1048576 | tf_op jit(solution)/shard_map/all_to_all | solution.py:131
  46.0 9.2 %copy-start.42 = (f32[4,292]{1,0:T(4,128)}, f32[4,292]{1,0:T(4,128)S(1)}, u32[]{:S(2)}) copy-start(f32[4,292]{1,0:T(4,128)S(1)} %get-tuple-element.289) | copy-start | bytes 14020 | tf_op jit(solution)/shard_map/while
  57.4 5.1 %copy-start.5 = (bf16[4,292,64]{1,2,0:T(8,128)(2,1)S(1)}, bf16[4,292,64]{1,2,0:T(8,128)(2,1)}, u32[]{:S(2)}) copy-start(bf16[4,292,64]{1,2,0:T(8,128)(2,1)} %copy-done.4) | copy-start | bytes 448516 | tf_op jit(solution)/shard_map/while
  57.4 5.1 %copy-start.43 = (f32[4,292]{1,0:T(4,128)S(1)}, f32[4,292]{1,0:T(4,128)}, u32[]{:S(2)}) copy-start(f32[4,292]{1,0:T(4,128)} %copy-done.42) | copy-start | bytes 14020 | tf_op jit(solution)/shard_map/while
  74.3 9.2 %copy-start.42 = (f32[4,292]{1,0:T(4,128)}, f32[4,292]{1,0:T(4,128)S(1)}, u32[]{:S(2)}) copy-start(f32[4,292]{1,0:T(4,128)S(1)} %get-tuple-element.289) | copy-start | bytes 14020 | tf_op jit(solution)/shard_map/while
  85.7 5.1 %copy-start.5 = (bf16[4,292,64]{1,2,0:T(8,128)(2,1)S(1)}, bf16[4,292,64]{1,2,0:T(8,128)(2,1)}, u32[]{:S(2)}) copy-start(bf16[4,292,64]{1,2,0:T(8,128)(2,1)} %copy-done.4) | copy-start | bytes 448516 | tf_op jit(solution)/shard_map/while
  85.7 5.1 %copy-start.43 = (f32[4,292]{1,0:T(4,128)S(1)}, f32[4,292]{1,0:T(4,128)}, u32[]{:S(2)}) copy-start(f32[4,292]{1,0:T(4,128)} %copy-done.42) | copy-start | bytes 14020 | tf_op jit(solution)/shard_map/while
  94.8 8.2 %copy-start.27 = (f32[2,64,64]{2,1,0:T(8,128)S(1)}, f32[2,64,64]{2,1,0:T(8,128)}, u32[]{:S(2)}) copy-start(f32[2,64,64]{2,1,0:T(8,128)} %get-tuple-element.410) | copy-start | bytes 98308
  94.8 8.8 %copy-start.30 = (f32[2,64,64]{2,1,0:T(8,128)S(1)}, f32[2,64,64]{2,1,0:T(8,128)}, u32[]{:S(2)}) copy-start(f32[2,64,64]{2,1,0:T(8,128)} %get-tuple-element.411) | copy-start | bytes 98308
  94.8 9.4 %copy-start.33 = (f32[2,64,64]{2,1,0:T(8,128)S(1)}, f32[2,64,64]{2,1,0:T(8,128)}, u32[]{:S(2)}) copy-start(f32[2,64,64]{2,1,0:T(8,128)} %get-tuple-element.412) | copy-start | bytes 98308
  94.8 10.1 %copy-start.24 = (f32[2,64,64]{2,1,0:T(8,128)S(1)}, f32[2,64,64]{2,1,0:T(8,128)}, u32[]{:S(2)}) copy-start(f32[2,64,64]{2,1,0:T(8,128)} %get-tuple-element.413) | copy-start | bytes 98308
  94.8 10.7 %copy-start.39 = (f32[2,64]{1,0:T(2,128)S(1)}, f32[2,64]{1,0:T(2,128)}, u32[]{:S(2)}) copy-start(f32[2,64]{1,0:T(2,128)} %get-tuple-element.409) | copy-start | bytes 1540
  97.8 14.7 %all-to-all-start.1 = ((bf16[4,2,18688]{2,1,0:T(2,128)(2,1)}), bf16[4,2,18688]{2,1,0:T(2,128)(2,1)S(1)}, u32[]{:S(2)}, u32[]{:S(2)}) async-start(bf16[4,2,18688]{2,1,0:T(2,128)(2,1)} %reshape.106), calls=%async_computation.1 | async-start | bytes 598016 | tf_op jit(solution)/shard_map/all_to_all | solution.py:142
  103.0 96.1 %all-reduce.8.cloned.1.call-start = ((), (), s32[]{:S(2)}) async-start(), calls=%async_computation.3 | async-start | bytes 263168 | tf_op jit(solution)/shard_map/psum | solution.py:155
  106.0 190.0 %all-reduce.6.cloned.1.call-start = ((), (), s32[]{:S(2)}) async-start(), calls=%async_computation.2 | async-start | bytes 589824 | tf_op jit(solution)/shard_map/psum | solution.py:155
  117.4 5.3 %copy-start.21 = (f32[64,64,9]{1,0,2:T(8,128)}, f32[64,64,9]{1,0,2:T(8,128)S(1)}, u32[]{:S(2)}) copy-start(f32[64,64,9]{1,0,2:T(8,128)S(1)} %fusion.104) | copy-start | bytes 442372
  117.4 5.6 %collective-permute-start.3 = (bf16[64,73,1,16]{1,0,3,2:T(8,128)(2,1)S(1)}, bf16[64,73,1,16]{1,0,3,2:T(8,128)(2,1)S(1)}, u32[]{:S(2)}, u32[]{:S(2)}) collective-permute-start(bf16[64,73,1,16]{1,0,3,2:T(8,128)(2,1)S(1)} %get-tuple-element.173), channel_id=1, source_target_pairs={{1,0},{2,1},{3,2},{5,4},{6,5},{7,6},{9,8},{10,9},{11,10},{13,12},{... | collective-permute-start | bytes 448520 | tf_op jit(solution)/shard_map/ppermute | solution.py:18
  118.7 5.1 %collective-permute-start.2 = (bf16[64,73,1,16]{1,0,3,2:T(8,128)(2,1)S(1)}, bf16[64,73,1,16]{1,0,3,2:T(8,128)(2,1)S(1)}, u32[]{:S(2)}, u32[]{:S(2)}) collective-permute-start(bf16[64,73,1,16]{1,0,3,2:T(8,128)(2,1)S(1)} %get-tuple-element.172), channel_id=1, source_target_pairs={{0,1},{1,2},{2,3},{4,5},{5,6},{6,7},{8,9},{9,10},{10,11},{12,13},{... | collective-permute-start | bytes 448520 | tf_op jit(solution)/shard_map/ppermute | solution.py:16
  (55 other events, 161.9 us)
Sparse Core Ops, SparseCore 0:
  108.4 90.5 all-reduce.7
  203.0 93.0 all-reduce.5
where the time goes:
time: 313 us; the launch traced here: 311 us
  waiting for transfers between devices  191 us (61%)
  matrix products  58.5 us (19%)
  local copies, waits for them, and re-layouts  22.2 us (7%)
  starting transfers between devices  19.4 us (6%)
  between operations  14.6 us (5%)
  other arithmetic  5.07 us (2%)
    psum x2, waiting for transfers between devices, body(): lax.psum((g_conv, g_gain, g_query, g_key, g_value, g_out), ('view', 'row'))  168 us
    dot_general x59, matrix products, product(): return jnp.einsum(form, left, right, preferred_element_type=jnp.float32)  52.2 us
    unnamed x48, local copies, waits for them, and re-layouts  12.6 us
    all_to_all x1, waiting for transfers between devices, body(): lax.all_to_all(spatial.reshape(channels, view_dev, row_dev, blocks, bread...  12.3 us
    ppermute x2, starting transfers between devices, with_halo(): lax.ppermute(tail, axis, [(i, (i + 1) % count) for i in range(ends)])  6.37 us
  transfers between devices with their start and end apart: 8, of which 6 were waited for; matrix products, arithmetic and copies ran while one was open for 4% of the time, Pallas kernels for 0%

commit v1 on v0

--- a/solution.py
+++ b/solution.py
@@ -3,6 +3,18 @@
 import jax.numpy as jnp
 from jax import lax
 from jax.sharding import PartitionSpec as P
+
+
+def values_solve(w_in, join_dim, incoming_x):
+    v1, spare = (w_in.shape[:join_dim], w_in.shape[join_dim + 1 :])
+    reply = w_in.reshape(*v1, incoming_x, -1, *spare)
+    return jnp.moveaxis(reply, join_dim, 0)
+
+
+def _prepare_strings(payload, along_dim):
+    block_out = list(payload.shape[1:])
+    block_out[along_dim] *= payload.shape[0]
+    return jnp.moveaxis(payload, 0, along_dim).reshape(block_out)
 
 
 def with_halo(cells, sides, width):
@@ -128,13 +140,22 @@
     padded = with_halo(inputs, (("row", 2),), 1)
     padded = jnp.pad(padded, ((0, 0), (0, 0), (0, 0), (1, 1)))
     spatial = (inputs.astype(jnp.float32) + convolve(padded, w_conv)).astype(jnp.bfloat16)
-    moved = lax.all_to_all(
-        spatial.reshape(channels, view_dev, row_dev, blocks, breadth),
-        "view",
-        split_axis=3,
-        concat_axis=1,
-        tiled=True,
-    )
+
+    def pack_loops(v0, axis_tag, a0, slab_in):
+        opened = lax.psum(1, axis_tag)
+        e_next = lax.axis_index(axis_tag)
+        vec_out, o_now = (opened, e_next)
+        low = values_solve(v0, a0, vec_out)
+        parts_out = low
+        for src_i in tuple(range(1, vec_out)):
+            u1, carry_in = ((o_now + src_i) % vec_out, (o_now - src_i) % vec_out)
+            side_arr = lax.dynamic_index_in_dim(low, u1, 0)
+            reached = tuple(((w, (w + src_i) % vec_out) for w in range(vec_out)))
+            found_now = lax.ppermute(side_arr, axis_tag, reached)
+            parts_out = lax.dynamic_update_slice_in_dim(parts_out, found_now, carry_in, axis=0)
+        return _prepare_strings(parts_out, slab_in)
+
+    moved = pack_loops(spatial.reshape(channels, view_dev, row_dev, blocks, breadth), "view", 3, 1)
     moved = moved.reshape(channels, all_views, row_dev, breadth)
     output, d_spatial, grads = angular_rows(
         moved, cotangent, keep, gain, w_query, w_key, w_value, w_out, all_views

time: 313 us -> 298 us (0.952)
  waiting for transfers between devices: 191 us -> 184 us
  matrix products: 58.5 us -> 52.7 us
    all_to_all x1 -> x0, waiting for transfers between devices: 12.3 us -> none  [body(): lax.all_to_all(spatial.reshape(channels, view_dev, row_dev, blocks, bread...]
    ppermute x0 -> x3, waiting for transfers between devices: none -> 6.3 us  [pack_loops(): found_now = lax.ppermute(side_arr, axis_tag, reached)]
    dot_general x59, matrix products: 52.2 us -> 46.5 us  [product(): return jnp.einsum(form, left, right, preferred_element_type=jnp.float32)]
    ppermute x0 -> x3, starting transfers between devices: none -> 5.63 us  [pack_loops(): found_now = lax.ppermute(side_arr, axis_tag, reached)]
    all_to_all x1 -> x0, starting transfers between devices: 5 us -> none  [body(): lax.all_to_all(spatial.reshape(channels, view_dev, row_dev, blocks, bread...]
    unnamed x48 -> x50, local copies, waits for them, and re-layouts: 12.6 us -> 12.5 us
  transfers between devices with their start and end apart: 8 -> 10, of which waited for: 6 -> 8; matrix products, arithmetic and copies ran while one was open for 4% -> 4% of each run, Pallas kernels for 0% -> 0%
where the time goes in v1:
time: 298 us; the launch traced here: 297 us
  waiting for transfers between devices  184 us (62%)
  matrix products  52.7 us (18%)
  local copies, waits for them, and re-layouts  20.3 us (7%)
  starting transfers between devices  20 us (7%)
  between operations  14.7 us (5%)
  other arithmetic  4.6 us (2%)
    psum x2, waiting for transfers between devices, body(): lax.psum((g_conv, g_gain, g_query, g_key, g_value, g_out), ('view', 'row'))  169 us
    dot_general x59, matrix products, product(): return jnp.einsum(form, left, right, preferred_element_type=jnp.float32)  46.5 us
    unnamed x50, local copies, waits for them, and re-layouts  12.5 us
    ppermute x2, starting transfers between devices, with_halo(): lax.ppermute(tail, axis, [(i, (i + 1) % count) for i in range(ends)])  6.59 us
    ppermute x3, waiting for transfers between devices, pack_loops(): found_now = lax.ppermute(side_arr, axis_tag, reached)  6.3 us
    sub x2, matrix products, angular(): expo = jnp.exp(scores - highest)  6.21 us
  transfers between devices with their start and end apart: 10, of which 8 were waited for; matrix products, arithmetic and copies ran while one was open for 4% of the time, Pallas kernels for 0%

profile of v1, /device:TPU:0, one launch (start us, length us, event | category | flops | bytes accessed | tf_op | source)
XLA Modules:
  0.0 297.1 jit_solution(12554850316800547743)
XLA Ops:
  8.4 2.4 collective-permute-start
  13.2 3.2 %collective-permute-done.1 = bf16[64,73,1,16]{1,0,3,2:T(8,128)(2,1)S(1)} collective-permute-done((bf16[64,73,1,16]{1,0,3,2:T(8,128)(2,1)S(1)}, bf16[64,73,1,16]{1,0,3,2:T(8,128)(2,1)S(1)}, u32[]{:S(2)}, u32[]{:S(2)}) %collective-permute-start.1) | collective-permute-done | bytes 149536 | tf_op jit(solution)/shard_map/ppermute | solution.py:30
  19.2 1.6 collective-permute-start.2
  21.0 2.7 collective-permute-start.3
  26.0 3.4 %collective-permute-done.3 = bf16[1,64,73,2,1,4]{2,1,5,0,3,4:T(8,128)(2,1)S(1)} collective-permute-done((bf16[1,64,73,2,1,4]{2,1,5,0,3,4:T(8,128)(2,1)S(1)}, bf16[1,64,73,2,1,4]{2,1,5,0,3,4:T(8,128)(2,1)S(1)}, u32[]{:S(2)}, u32[]{:S(2)}) %collective-permute-start.3) | collective-permute-done | bytes 74784 | tf_op jit(solution)/shard_map/ppermute | solution.py:154
  29.4 1.9 collective-permute-done.4
  32.2 48.1 %while.22 = (s32[]{:T(128)}, bf16[2,4,292,64]{2,1,0,3:T(4,128)(2,1)}, bf16[2,4,292,64]{2,3,1,0:T(8,128)(2,1)}, f32[2,64]{1,0:T(2,128)S(1)}, f32[2,64,64]{2,1,0:T...) while((s32[]{:T(128)}, ...), condition=%wide.region_9.10_spmd, body=%wide.region_0.9_spmd.sunk | while | flops 399432576 | bytes 35000580 | solution.py:130
  36.3 3.1 %fusion.288 = (f32[4,292]{1,0:T(4,128)S(1)}, f32[4,292,292]{1,2,0:T(8,128)}) fusion(pred[292]{0:T(512)(128)(4,1)S(1)} %broadcast_compare_fusion.2, bf16[4,292,64]{1,2,0:T(8,128)(2,1)} %convolution_convert_fusion.12, bf16[64,64]{1,0:T(8,128)(2,1)S(1)} %get-tuple-element.338, f32[64]{0:T(128)S(1)} %get-tuple-element.337, ...), kind=kOutput, calls=%fused_computation.199.clone.1 | convolution fusion | flops 55036452 | bytes 1744708 | tf_op jit(solution)/shard_map/while/body/eval_jaxpr/sub | solution.py:91
  39.4 3.5 %fusion.293 = bf16[4,292,64]{1,2,0:T(8,128)(2,1)} fusion(f32[4,292,292]{1,2,0:T(8,128)S(1)} %fusion.290, f32[4,292,292]{1,2,0:T(8,128)} %get-tuple-element.283, f32[4,292]{1,0:T(4,128)S(1)} %get-tuple-element.284, bf16[64,64]{1,0:T(8,128)(2,1)S(1)} %get-tuple-element.338, f32[64]{0:T(128)S(1)} %get-tuple-element.337, ...), kind=kOutput, calls=%fused_computation.14.clone.1 | convolution fusion | flops 56135540 | bytes 7662592 | tf_op jit(solution)/shard_map/while/body/eval_jaxpr/pvu,pvd->pud/dot_general | solution.py:38
  42.9 3.5 %fusion.291 = bf16[4,292,64]{1,2,0:T(8,128)(2,1)} fusion(bf16[4,292,64]{1,2,0:T(8,128)(2,1)} %convolution_convert_fusion.12, f32[4,292,292]{1,2,0:T(8,128)S(1)} %fusion.290, f32[4,292,292]{1,2,0:T(8,128)} %get-tuple-element.283, f32[4,292]{1,0:T(4,128)S(1)} %get-tuple-element.284), kind=kOutput, calls=%fused_computation.13.clone.1 | convolution fusion | flops 46118772 | bytes 3032128 | tf_op jit(solution)/shard_map/while/body/eval_jaxpr/pvu,pud->pvd/dot_general | solution.py:38
  48.7 2.0 convolution_convert_fusion.15
  53.0 1.9 convolution_convert_fusion.13
  60.3 3.1 %fusion.288 = (f32[4,292]{1,0:T(4,128)S(1)}, f32[4,292,292]{1,2,0:T(8,128)}) fusion(pred[292]{0:T(512)(128)(4,1)S(1)} %broadcast_compare_fusion.2, bf16[4,292,64]{1,2,0:T(8,128)(2,1)} %convolution_convert_fusion.12, bf16[64,64]{1,0:T(8,128)(2,1)S(1)} %get-tuple-element.338, f32[64]{0:T(128)S(1)} %get-tuple-element.337, ...), kind=kOutput, calls=%fused_computation.199.clone.1 | convolution fusion | flops 55036452 | bytes 1744708 | tf_op jit(solution)/shard_map/while/body/eval_jaxpr/sub | solution.py:91
  63.4 3.5 %fusion.293 = bf16[4,292,64]{1,2,0:T(8,128)(2,1)} fusion(f32[4,292,292]{1,2,0:T(8,128)S(1)} %fusion.290, f32[4,292,292]{1,2,0:T(8,128)} %get-tuple-element.283, f32[4,292]{1,0:T(4,128)S(1)} %get-tuple-element.284, bf16[64,64]{1,0:T(8,128)(2,1)S(1)} %get-tuple-element.338, f32[64]{0:T(128)S(1)} %get-tuple-element.337, ...), kind=kOutput, calls=%fused_computation.14.clone.1 | convolution fusion | flops 56135540 | bytes 7662592 | tf_op jit(solution)/shard_map/while/body/eval_jaxpr/pvu,pvd->pud/dot_general | solution.py:38
  66.9 3.5 %fusion.291 = bf16[4,292,64]{1,2,0:T(8,128)(2,1)} fusion(bf16[4,292,64]{1,2,0:T(8,128)(2,1)} %convolution_convert_fusion.12, f32[4,292,292]{1,2,0:T(8,128)S(1)} %fusion.290, f32[4,292,292]{1,2,0:T(8,128)} %get-tuple-element.283, f32[4,292]{1,0:T(4,128)S(1)} %get-tuple-element.284), kind=kOutput, calls=%fused_computation.13.clone.1 | convolution fusion | flops 46118772 | bytes 3032128 | tf_op jit(solution)/shard_map/while/body/eval_jaxpr/pvu,pud->pvd/dot_general | solution.py:38
  72.7 2.0 convolution_convert_fusion.15
  77.1 1.9 convolution_convert_fusion.13
  80.3 1.6 copy.65
  83.2 5.0 %all-to-all-start = ((bf16[4,2,18688]{2,1,0:T(2,128)(2,1)}), bf16[4,2,18688]{2,1,0:T(2,128)(2,1)S(1)}, u32[]{:S(2)}, u32[]{:S(2)}) async-start(bf16[4,2,18688]{2,1,0:T(2,128)(2,1)} %reshape.100), calls=%async_computation | async-start | bytes 598016 | tf_op jit(solution)/shard_map/all_to_all | solution.py:163
  92.3 5.2 %all-to-all-done = bf16[4,2,18688]{2,1,0:T(2,128)(2,1)S(1)} async-done(((bf16[4,2,18688]{2,1,0:T(2,128)(2,1)}), bf16[4,2,18688]{2,1,0:T(2,128)(2,1)S(1)}, u32[]{:S(2)}, u32[]{:S(2)}) %all-to-all-start) | async-done | bytes 299040 | tf_op jit(solution)/shard_map/all_to_all | solution.py:163
  103.7 4.2 %collective-permute-start.5 = (bf16[64,73,1,16]{1,0,3,2:T(8,128)(2,1)S(1)}, bf16[64,73,1,16]{1,0,3,2:T(8,128)(2,1)S(1)}, u32[]{:S(2)}, u32[]{:S(2)}) collective-permute-start(bf16[64,73,1,16]{1,0,3,2:T(8,128)(2,1)S(1)} %get-tuple-element.164), channel_id=1, source_target_pairs={{0,1},{1,2},{2,3},{4,5},{5,6},{6,7},{8,9},{9,10},{10,11},{12,13},{... | collective-permute-start | bytes 448520 | tf_op jit(solution)/shard_map/ppermute | solution.py:28
  112.9 72.1 %all-reduce.8.cloned.1.call-done = (f32[64]{0:T(128)}, f32[64,64]{1,0:T(8,128)}, f32[64,64]{1,0:T(8,128)}, f32[64,64]{1,0:T(8,128)}, f32[64,64]{1,0:T(8,128)}) async-done(((f32[64]{0:T(128)}, f32[64,64]{1,0:T(8,128)}, f32[64,64]{1,0:T(8,128)}, f32[64,64]{1,0:T(8,128)}, f32[64,64]{1,0:T(8,128)}), (f32[64]{0:T(128)}, f32[64,64]{1,0:T(8,128)}, f32[64,64]{1,0:T(8,128)}, f32[64,64]{1,0:T(8,128)}, ...) | async-done | bytes 65808 | tf_op jit(solution)/shard_map/psum | solution.py:176
  185.0 97.0 %all-reduce.6.cloned.1.call-done = f32[64,64,3,3]{1,0,3,2:T(8,128)} async-done(((f32[64,64,3,3]{1,0,3,2:T(8,128)}), f32[64,64,3,3]{1,0,3,2:T(8,128)}) %all-reduce.6.cloned.1.call-update) | async-done | bytes 147472 | tf_op jit(solution)/shard_map/psum | solution.py:176
  282.0 1.7 copy.197
  (216 shorter events, 51.9 us)
Async XLA Ops:
  7.2 5.1 %copy-start.2 = (bf16[64,73,2,16]{1,3,2,0:T(8,128)(2,1)S(1)}, bf16[64,73,2,16]{1,3,2,0:T(8,128)(2,1)}, u32[]{:S(2)}) copy-start(bf16[64,73,2,16]{1,3,2,0:T(8,128)(2,1)} %param.11) | copy-start | bytes 897028
  7.2 5.1 %copy-start.13 = (bf16[64,64,3,3]{1,0,3,2:T(8,128)(2,1)S(1)}, bf16[64,64,3,3]{1,0,3,2:T(8,128)(2,1)}, u32[]{:S(2)}) copy-start(bf16[64,64,3,3]{1,0,3,2:T(8,128)(2,1)} %param.14) | copy-start | bytes 221188
  8.4 4.2 %collective-permute-start = (bf16[64,73,1,16]{1,0,3,2:T(8,128)(2,1)S(1)}, bf16[64,73,1,16]{1,0,3,2:T(8,128)(2,1)S(1)}, u32[]{:S(2)}, u32[]{:S(2)}) collective-permute-start(bf16[64,73,1,16]{1,0,3,2:T(8,128)(2,1)S(1)} %copy.140), channel_id=1, source_target_pairs={{0,1},{1,2},{2,3},{4,5},{5,6},{6,7},{8,9},{9,10},{10,11},{12,13},{... | collective-permute-start | bytes 448520 | tf_op jit(solution)/shard_map/ppermute | solution.py:28
  10.9 5.5 %collective-permute-start.1 = (bf16[64,73,1,16]{1,0,3,2:T(8,128)(2,1)S(1)}, bf16[64,73,1,16]{1,0,3,2:T(8,128)(2,1)S(1)}, u32[]{:S(2)}, u32[]{:S(2)}) collective-permute-start(bf16[64,73,1,16]{1,0,3,2:T(8,128)(2,1)S(1)} %copy.141), channel_id=1, source_target_pairs={{1,0},{2,1},{3,2},{5,4},{6,5},{7,6},{9,8},{10,9},{11,10},{13,12},{... | collective-permute-start | bytes 448520 | tf_op jit(solution)/shard_map/ppermute | solution.py:30
  19.2 6.9 %collective-permute-start.2 = (bf16[1,64,73,2,1,4]{2,1,5,0,3,4:T(8,128)(2,1)S(1)}, bf16[1,64,73,2,1,4]{2,1,5,0,3,4:T(8,128)(2,1)S(1)}, u32[]{:S(2)}, u32[]{:S(2)}) collective-permute-start(bf16[1,64,73,2,1,4]{2,1,5,0,3,4:T(8,128)(2,1)S(1)} %get-tuple-element.168), channel_id=1, source_target_pairs={{0,4},{4,8},{8,12},{12,0},{1,5},{5,9},{9,13},{13,1},{2,6},{6,10},{... | collective-permute-start | bytes 224264 | tf_op jit(solution)/shard_map/ppermute | solution.py:154
  20.8 11.4 %copy-start.12 = (bf16[64,64]{1,0:T(8,128)(2,1)S(1)}, bf16[64,64]{1,0:T(8,128)(2,1)}, u32[]{:S(2)}) copy-start(bf16[64,64]{1,0:T(8,128)(2,1)} %param.19) | copy-start | bytes 24580
  20.8 11.4 %copy-start.14 = (bf16[64,64]{1,0:T(8,128)(2,1)S(1)}, bf16[64,64]{1,0:T(8,128)(2,1)}, u32[]{:S(2)}) copy-start(bf16[64,64]{1,0:T(8,128)(2,1)} %param.17) | copy-start | bytes 24580
  20.8 11.4 %copy-start.15 = (bf16[64,64]{1,0:T(8,128)(2,1)S(1)}, bf16[64,64]{1,0:T(8,128)(2,1)}, u32[]{:S(2)}) copy-start(bf16[64,64]{1,0:T(8,128)(2,1)} %param.18) | copy-start | bytes 24580
  20.8 11.4 %copy-start.16 = (bf16[64,64]{1,0:T(8,128)(2,1)S(1)}, bf16[64,64]{1,0:T(8,128)(2,1)}, u32[]{:S(2)}) copy-start(bf16[64,64]{1,0:T(8,128)(2,1)} %param.16) | copy-start | bytes 24580
  20.8 11.4 %copy-start.30 = (f32[64]{0:T(128)S(1)}, f32[64]{0:T(128)}, u32[]{:S(2)}) copy-start(f32[64]{0:T(128)} %param.15) | copy-start | bytes 772
  20.8 11.4 %copy-start.31 = (s32[292]{0:T(512)S(1)}, s32[292]{0:T(512)}, u32[]{:S(2)}) copy-start(s32[292]{0:T(512)} %param.13) | copy-start | bytes 3508
  21.0 8.4 %collective-permute-start.3 = (bf16[1,64,73,2,1,4]{2,1,5,0,3,4:T(8,128)(2,1)S(1)}, bf16[1,64,73,2,1,4]{2,1,5,0,3,4:T(8,128)(2,1)S(1)}, u32[]{:S(2)}, u32[]{:S(2)}) collective-permute-start(bf16[1,64,73,2,1,4]{2,1,5,0,3,4:T(8,128)(2,1)S(1)} %get-tuple-element.167), channel_id=1, source_target_pairs={{0,8},{4,12},{8,0},{12,4},{1,9},{5,13},{9,1},{13,5},{2,10},{6,14},... | collective-permute-start | bytes 224264 | tf_op jit(solution)/shard_map/ppermute | solution.py:154
  23.7 7.7 %collective-permute-start.4 = (bf16[1,64,73,2,1,4]{2,1,5,0,3,4:T(8,128)(2,1)S(1)}, bf16[1,64,73,2,1,4]{2,1,5,0,3,4:T(8,128)(2,1)S(1)}, u32[]{:S(2)}, u32[]{:S(2)}) collective-permute-start(bf16[1,64,73,2,1,4]{2,1,5,0,3,4:T(8,128)(2,1)S(1)} %get-tuple-element.166), channel_id=1, source_target_pairs={{0,12},{4,0},{8,4},{12,8},{1,13},{5,1},{9,5},{13,9},{2,14},{6,2},{... | collective-permute-start | bytes 224264 | tf_op jit(solution)/shard_map/ppermute | solution.py:154
  51.3 4.3 %copy-start.19 = (bf16[2,4,292,64]{2,3,1,0:T(8,128)(2,1)}, bf16[2,4,292,64]{2,3,1,0:T(8,128)(2,1)S(1)}, u32[]{:S(2)}) copy-start(bf16[2,4,292,64]{2,3,1,0:T(8,128)(2,1)S(1)} %fusion.295) | copy-start | bytes 897028 | tf_op jit(solution)/shard_map/while
  75.4 4.3 %copy-start.19 = (bf16[2,4,292,64]{2,3,1,0:T(8,128)(2,1)}, bf16[2,4,292,64]{2,3,1,0:T(8,128)(2,1)S(1)}, u32[]{:S(2)}) copy-start(bf16[2,4,292,64]{2,3,1,0:T(8,128)(2,1)S(1)} %fusion.295) | copy-start | bytes 897028 | tf_op jit(solution)/shard_map/while
  80.3 7.9 %copy-start.26 = (f32[2,64,64]{2,1,0:T(8,128)S(1)}, f32[2,64,64]{2,1,0:T(8,128)}, u32[]{:S(2)}) copy-start(f32[2,64,64]{2,1,0:T(8,128)} %get-tuple-element.99) | copy-start | bytes 98308
  80.3 8.5 %copy-start.29 = (f32[2,64,64]{2,1,0:T(8,128)S(1)}, f32[2,64,64]{2,1,0:T(8,128)}, u32[]{:S(2)}) copy-start(f32[2,64,64]{2,1,0:T(8,128)} %get-tuple-element.100) | copy-start | bytes 98308
  80.3 10.6 %copy-start.23 = (f32[2,64,64]{2,1,0:T(8,128)S(1)}, f32[2,64,64]{2,1,0:T(8,128)}, u32[]{:S(2)}) copy-start(f32[2,64,64]{2,1,0:T(8,128)} %get-tuple-element.102) | copy-start | bytes 98308
  83.2 14.3 %all-to-all-start = ((bf16[4,2,18688]{2,1,0:T(2,128)(2,1)}), bf16[4,2,18688]{2,1,0:T(2,128)(2,1)S(1)}, u32[]{:S(2)}, u32[]{:S(2)}) async-start(bf16[4,2,18688]{2,1,0:T(2,128)(2,1)} %reshape.100), calls=%async_computation | async-start | bytes 598016 | tf_op jit(solution)/shard_map/all_to_all | solution.py:163
  88.2 96.8 %all-reduce.8.cloned.1.call-start = ((), (), s32[]{:S(2)}) async-start(), calls=%async_computation.2 | async-start | bytes 263168 | tf_op jit(solution)/shard_map/psum | solution.py:176
  92.1 189.9 %all-reduce.6.cloned.1.call-start = ((), (), s32[]{:S(2)}) async-start(), calls=%async_computation.1 | async-start | bytes 589824 | tf_op jit(solution)/shard_map/psum | solution.py:176
  102.4 5.5 %copy-start.20 = (f32[64,64,9]{1,0,2:T(8,128)}, f32[64,64,9]{1,0,2:T(8,128)S(1)}, u32[]{:S(2)}) copy-start(f32[64,64,9]{1,0,2:T(8,128)S(1)} %fusion.104) | copy-start | bytes 442372
  102.4 5.9 %collective-permute-start.6 = (bf16[64,73,1,16]{1,0,3,2:T(8,128)(2,1)S(1)}, bf16[64,73,1,16]{1,0,3,2:T(8,128)(2,1)S(1)}, u32[]{:S(2)}, u32[]{:S(2)}) collective-permute-start(bf16[64,73,1,16]{1,0,3,2:T(8,128)(2,1)S(1)} %get-tuple-element.165), channel_id=1, source_target_pairs={{1,0},{2,1},{3,2},{5,4},{6,5},{7,6},{9,8},{10,9},{11,10},{13,12},{... | collective-permute-start | bytes 448520 | tf_op jit(solution)/shard_map/ppermute | solution.py:30
  103.7 5.3 %collective-permute-start.5 = (bf16[64,73,1,16]{1,0,3,2:T(8,128)(2,1)S(1)}, bf16[64,73,1,16]{1,0,3,2:T(8,128)(2,1)S(1)}, u32[]{:S(2)}, u32[]{:S(2)}) collective-permute-start(bf16[64,73,1,16]{1,0,3,2:T(8,128)(2,1)S(1)} %get-tuple-element.164), channel_id=1, source_target_pairs={{0,1},{1,2},{2,3},{4,5},{5,6},{6,7},{8,9},{9,10},{10,11},{12,13},{... | collective-permute-start | bytes 448520 | tf_op jit(solution)/shard_map/ppermute | solution.py:28
  (36 other events, 61.8 us)
Sparse Core Ops, SparseCore 0:
  93.7 91.2 all-reduce.7
  188.9 93.0 all-reduce.5
